TPU v7x, 512 devices: a whole 4x4x16 slice. The times are simulated.
512 devices in a mesh: mode: 64 (over y, z), rank: 8 (over x, core).
Axes of the slice: x: 4, y: 4, z: 16, core: 2. Of those that a mesh axis runs over, the one named last changes fastest.
Arguments:
- operator_cores: bfloat16 [2, 4, 4, 2048, 2048], P(None, None, None, 'mode'), may hold values from -0.26516504 to 0.26516504
- vector_cores: bfloat16 [2, 64, 64, 2048], P(None, 'rank', None, 'mode'), may hold values from -17 to 17
- left_gram: float32 [256, 256], replicated, may hold values from -330 to 330, as said below
- bases: float32 [3, 256, 64], replicated, may hold values from -0.375 to 0.375
Outputs:
- rounded_cores: float32 [2, 64, 2048, 64], P(None, None, ('mode', 'rank'))
- final_gram: float32 [256, 256], replicated
Inputs may be any that keep to these rules, and one draw needn't show every extreme that they name: left_gram is symmetric positive definite.
All inputs are finite; a program needn't handle non-finite values.
Results may differ from a plain program's by a relative error of at most 0.0028.
Values may be sent and summed in bfloat16 or wider, within the bound.
A program may use at most 64 MiB of HBM per device.

v0:
```python
import jax
import jax.numpy as jnp
from jax import lax
from jax.sharding import PartitionSpec as P

MODES = 2048
RANK = 256


HIGHEST_PRECISION = lax.Precision.HIGHEST


def solve_mixing(gram_now, basis):
    projected = jnp.dot(
        basis.T, gram_now, precision=HIGHEST_PRECISION, preferred_element_type=jnp.float32
    )
    reduced = jnp.dot(
        projected, basis, precision=HIGHEST_PRECISION, preferred_element_type=jnp.float32
    )
    reduced = 0.5 * (reduced + reduced.T)
    lower_factor = jnp.linalg.cholesky(reduced)
    return jax.scipy.linalg.cho_solve((lower_factor, True), projected)


def shards(operator_cores, vector_cores, left_gram, bases):
    gram_now = left_gram
    results = []
    core_count = operator_cores.shape[0]
    for core_index in range(core_count):
        mixing = solve_mixing(gram_now, bases[core_index])
        next_basis = bases[core_index + 1]
        operator_core = operator_cores[core_index]
        vector_core = vector_cores[core_index]
        local_rows = vector_core.shape[0]
        vector_width = vector_core.shape[1]
        operator_width = operator_core.shape[0]
        local_modes = operator_core.shape[2]
        gathered = lax.all_gather(vector_core, "mode", axis=2, tiled=True)
        product = jnp.einsum(
            "qsj,ptij->qpist", gathered, operator_core, preferred_element_type=jnp.float32
        )
        row_major = product.reshape(
            local_rows * operator_width, local_modes, vector_width * operator_width
        )
        row_major = row_major.astype(jnp.bfloat16)
        exchanged = lax.all_to_all(row_major, "rank", split_axis=1, concat_axis=0, tiled=True)
        widened = exchanged.astype(jnp.float32)
        weighted = jnp.einsum("ad,dib->aib", gram_now, widened, precision=HIGHEST_PRECISION)
        partial_gram = jnp.einsum("aib,aic->bc", widened, weighted, precision=HIGHEST_PRECISION) / (
            MODES * RANK
        )
        mixed = jnp.einsum("sa,aib->sib", mixing, widened, precision=HIGHEST_PRECISION)
        rounded_core = jnp.einsum("sib,bt->sit", mixed, next_basis, precision=HIGHEST_PRECISION)
        results.append(rounded_core)
        gram_now = lax.psum(partial_gram, ("mode", "rank"))
    return (jnp.stack(results), gram_now)


def solution(mesh):
    placed = (P(None, None, None, "mode", None), P(None, "rank", None, "mode"), P(), P())
    return jax.shard_map(
        shards,
        mesh=mesh,
        in_specs=placed,
        out_specs=(P(None, None, ("mode", "rank"), None), P()),
        check_vma=False,
    )
```

profile of v0, /device:TPU:1, one launch (start us, length us, event | category | flops | bytes accessed | tf_op | source)
XLA Modules:
  0.0 1262.8 jit_solution(10983501923882909832)
XLA Ops:
  7.2 0.9 fusion.62
  8.1 0.7 copy.55
  8.9 0.7 copy.56
  9.6 1.1 fusion.43
  10.7 1.0 fusion.41
  11.8 0.1 copy.29
  11.9 5.8 cholesky.44
  17.8 0.7 compare_reduce_fusion.1
  18.5 0.6 fusion.51
  19.1 4.9 custom-call.8
  24.0 0.3 fusion.58
  24.3 0.2 convolution_bitcast_fusion.6
  24.5 130.9 %all-gather.5.cloned.1.call-done = bf16[1,8,64,2048]{2,1,0,3:T(8,128)(2,1)} async-done(((bf16[1,8,64,32]{2,1,0,3:T(8,128)(2,1)}), bf16[1,8,64,2048]{2,1,0,3:T(8,128)(2,1)}) %all-gather.5.cloned.1.call-update) | async-done | bytes 2097168 | tf_op jit(solution)/shard_map/all_gather | solution.py:38
  155.4 4.5 copy.31
  159.8 3.9 fusion.23
  163.8 1.4 copy.32
  165.1 1.8 copy.33
  166.9 13.1 %all-to-all-start = ((bf16[32,32,256]{2,0,1:T(8,128)(2,1)}), bf16[32,32,256]{2,0,1:T(8,128)(2,1)S(1)}, u32[]{:S(2)}, u32[]{:S(2)}) async-start(bf16[32,32,256]{2,0,1:T(8,128)(2,1)} %copy.33), calls=%async_computation | async-start | bytes 1048576 | tf_op jit(solution)/shard_map/all_to_all | solution.py:46
  180.0 120.1 %all-gather.7.cloned.1.call-done = bf16[1,8,64,2048]{2,1,0,3:T(8,128)(2,1)} async-done(((bf16[1,8,64,32]{2,1,0,3:T(8,128)(2,1)}), bf16[1,8,64,2048]{2,1,0,3:T(8,128)(2,1)}) %all-gather.7.cloned.1.call-update) | async-done | bytes 2097168 | tf_op jit(solution)/shard_map/all_gather | solution.py:38
  300.1 4.5 copy.41
  304.6 4.9 fusion.18
  309.5 2.9 copy.42
  312.4 1.8 copy.43
  314.2 13.0 %all-to-all-start.1 = ((bf16[32,32,256]{2,0,1:T(8,128)(2,1)}), bf16[32,32,256]{2,0,1:T(8,128)(2,1)S(1)}, u32[]{:S(2)}, u32[]{:S(2)}) async-start(bf16[32,32,256]{2,0,1:T(8,128)(2,1)} %copy.43), calls=%async_computation.1 | async-start | bytes 1048576 | tf_op jit(solution)/shard_map/all_to_all | solution.py:46
  327.3 0.7 convolution_bitcast_fusion
  328.0 1.5 fusion.29
  329.5 0.2 all-reduce.5.cloned.1.call-start
  329.7 0.4 fusion.63
  330.1 6.6 all-to-all-done.1
  336.8 0.4 convolution_bitcast_fusion.4
  337.1 447.2 %all-reduce.3.cloned.1.call-done = f32[256,256]{1,0:T(8,128)} async-done(((f32[256,256]{1,0:T(8,128)}), f32[256,256]{1,0:T(8,128)}) %all-reduce.3.cloned.1.call-update) | async-done | bytes 262160 | tf_op jit(solution)/shard_map/psum | solution.py:55
  784.3 1.3 fusion.37
  785.6 0.2 fusion.39
  785.8 0.1 copy.38
  785.9 0.1 copy.39
  786.0 5.8 cholesky.55
  791.9 0.6 compare_reduce_fusion
  792.5 0.7 fusion.52
  793.2 4.9 custom-call.9
  798.1 0.3 fusion.34
  798.4 0.2 convolution_bitcast_fusion.5
  798.6 0.4 fusion.64
  798.9 0.6 fusion.30
  799.5 1.5 fusion.28
  801.1 0.4 convolution_bitcast_fusion.3
  801.4 0.9 copy.46
  802.3 452.2 %all-reduce.5.cloned.1.call-done = f32[256,256]{1,0:T(8,128)} async-done(((f32[256,256]{1,0:T(8,128)}), f32[256,256]{1,0:T(8,128)}) %all-reduce.5.cloned.1.call-update) | async-done | bytes 262160 | tf_op jit(solution)/shard_map/psum | solution.py:55
  1254.6 1.7 copy.59
  (24 shorter events, 0.5 us)
Async XLA Ops:
  7.2 2.4 copy-start
  7.2 148.2 %all-gather.5.cloned.1.call-start = ((), (), s32[]{:S(2)}) async-start(), calls=%async_computation.4 | async-start | bytes 4259840 | tf_op jit(solution)/shard_map/all_gather | solution.py:38
  8.8 291.3 %all-gather.7.cloned.1.call-start = ((), (), s32[]{:S(2)}) async-start(), calls=%async_computation.5 | async-start | bytes 4259840 | tf_op jit(solution)/shard_map/all_gather | solution.py:38
  166.9 147.2 %all-to-all-start = ((bf16[32,32,256]{2,0,1:T(8,128)(2,1)}), bf16[32,32,256]{2,0,1:T(8,128)(2,1)S(1)}, u32[]{:S(2)}, u32[]{:S(2)}) async-start(bf16[32,32,256]{2,0,1:T(8,128)(2,1)} %copy.33), calls=%async_computation | async-start | bytes 1048576 | tf_op jit(solution)/shard_map/all_to_all | solution.py:46
  314.2 22.5 %all-to-all-start.1 = ((bf16[32,32,256]{2,0,1:T(8,128)(2,1)}), bf16[32,32,256]{2,0,1:T(8,128)(2,1)S(1)}, u32[]{:S(2)}, u32[]{:S(2)}) async-start(bf16[32,32,256]{2,0,1:T(8,128)(2,1)} %copy.43), calls=%async_computation.1 | async-start | bytes 1048576 | tf_op jit(solution)/shard_map/all_to_all | solution.py:46
  327.2 457.1 %all-reduce.3.cloned.1.call-start = ((), (), s32[]{:S(2)}) async-start(), calls=%async_computation.2 | async-start | bytes 524288 | tf_op jit(solution)/shard_map/psum | solution.py:55
  328.0 8.8 copy-start.2
  329.5 925.0 %all-reduce.5.cloned.1.call-start = ((), (), s32[]{:S(2)}) async-start(), calls=%async_computation.3 | async-start | bytes 524288 | tf_op jit(solution)/shard_map/psum | solution.py:55
  784.3 14.6 %copy-start.1 = (f32[256,256]{1,0:T(8,128)S(1)}, f32[256,256]{1,0:T(8,128)}, u32[]{:S(2)}) copy-start(f32[256,256]{1,0:T(8,128)} %all-reduce.3.cloned.1.call-done) | copy-start | bytes 786436
Sparse Core Ops, SparseCore 0:
  11.5 143.7 all-gather.4
  158.9 141.1 all-gather.6
  334.1 450.1 all-reduce.2
  801.2 453.3 all-reduce.4
where the time goes:
time: 1260 us
  waiting for transfers between devices  1160 us (92%)
  starting transfers between devices  26.4 us (2%)
  other arithmetic  24.2 us (2%)
  local copies, waits for them, and re-layouts  21.9 us (2%)
  matrix products  19.1 us (2%)
  between operations  14 us (1%)
    psum x2, waiting for transfers between devices, shards(): gram_now = lax.psum(partial_gram, ('mode', 'rank'))  899 us
    all_gather x2, waiting for transfers between devices, shards(): gathered = lax.all_gather(vector_core, 'mode', axis=2, tiled=True)  251 us
    all_to_all x2, starting transfers between devices, shards(): lax.all_to_all(row_major, 'rank', split_axis=1, concat_axis=0, tiled=True)  26.1 us
  transfers between devices with their start and end apart: 6, of which 5 were waited for; matrix products, arithmetic and copies ran while one was open for 4% of the time, Pallas kernels for 0%

commit v1 on v0

v1 whole, which is shorter than its diff:
```python
import functools

import jax
import jax.numpy as jnp
from jax import lax
from jax.experimental import pallas as pl
from jax.experimental.pallas import tpu as pltpu
from jax.sharding import PartitionSpec as P

GRID_Y = 4
HIGHEST_PRECISION = lax.Precision.HIGHEST
MESH = pl.DeviceIdType.MESH
F32 = jnp.float32
BF16 = jnp.bfloat16


def solve_mixing(gram_now, basis):
    projected = jnp.dot(
        basis.T, gram_now, precision=HIGHEST_PRECISION, preferred_element_type=jnp.float32
    )
    reduced = jnp.dot(
        projected, basis, precision=HIGHEST_PRECISION, preferred_element_type=jnp.float32
    )
    reduced = 0.5 * (reduced + reduced.T)
    lower_factor = jnp.linalg.cholesky(reduced)
    return jax.scipy.linalg.cho_solve((lower_factor, True), projected)


def mm(a, b):
    return jnp.dot(a, b, preferred_element_type=F32)


def mm_nt(a, b):
    return lax.dot_general(a, b, (((1,), (1,)), ((), ())), preferred_element_type=F32)


def split(a):
    high = a.astype(BF16)
    return high, (a - high.astype(F32)).astype(BF16)


def one_hot(shape, target):
    rows = lax.broadcasted_iota(jnp.int32, shape, 0)
    columns = lax.broadcasted_iota(jnp.int32, shape, 1)
    return jnp.where(target(rows) == columns, 1.0, 0.0).astype(BF16)


def window_kernel(dims, *refs):
    (ny, nz, nr, lm, ql, vw, ow, rank) = dims
    (v_ref, o_hbm, g_ref, b_ref, q_out, gram_out,
     o_buf, vg, acc, s_buf, x_buf, y_buf, p_buf, pt_buf, part, ra, sb, rb, gram,
     o_sem, ys0, yr0, zs0, zr0, zs1, zr1, ys1, yr1, as_sem, ar_sem,
     a_s, a_r, b_s, b_r, c_s, c_r) = refs
    modes = ny * nz * lm
    ni = lm // nr
    rows = ow * ow * lm
    chunk = ow * ni
    no = ny * nr
    rb_rows = rank // no
    kr = nz // 2
    kl = nz - 1 - kr
    mode = lax.axis_index("mode")
    r = lax.axis_index("rank")
    y = mode // nz
    z = mode % nz
    o = y * nr + r
    right, left = (z + 1) % nz, (z + nz - 1) % nz

    def group(k):
        other = (o + k) % no
        return other, ((other // nr) * nz + z, other % nr)

    def group_from(k):
        return (o + no - k) % no

    o_copies = [
        pltpu.make_async_copy(o_hbm.at[c], o_buf.at[c], o_sem.at[c]) for c in range(2)
    ]
    for copy in o_copies:
        copy.start()

    barrier = pltpu.get_barrier_semaphore()

    def greet_group(k, carry):
        pl.semaphore_signal(barrier, inc=1, device_id=group(k)[1], device_id_type=MESH)
        return carry

    def greet_z(k, carry):
        pl.semaphore_signal(
            barrier, inc=1, device_id=(y * nz + (z + k) % nz, r), device_id_type=MESH
        )
        return carry

    lax.fori_loop(1, no, greet_group, 0)
    lax.fori_loop(1, nz, greet_z, 0)

    def block(yy, zz):
        return pl.ds(pl.multiple_of((yy * nz + zz) * lm, lm), lm)

    eye = one_hot((lm, lm), lambda i: i)
    for c in range(2):
        vg[c, block(y, z), :] = mm_nt(eye, v_ref[c]).astype(BF16)

    def operator_row(i):
        rr, rest = i // (ow * chunk), i % (ow * chunk)
        t, rest = rest // chunk, rest % chunk
        p, ii = rest // ni, rest % ni
        return (p * ow + t) * lm + rr * ni + ii

    width = min(256, modes)
    order = one_hot((rows, rows), operator_row)
    for c in range(2):
        o_copies[c].wait()

        def reorder(n, carry, c=c):
            columns = pl.ds(pl.multiple_of(n * width, width), width)
            o_buf[c, :, columns] = mm(order, o_buf[c, :, columns]).astype(BF16)
            return carry

        lax.fori_loop(0, modes // width, reorder, 0)

    pl.semaphore_wait(barrier, no - 1 + nz - 1)

    def send(src, dst, ssem, rsem, device):
        return pltpu.make_async_remote_copy(
            src_ref=src, dst_ref=dst, send_sem=ssem, recv_sem=rsem,
            device_id=device, device_id_type=MESH,
        )

    def y_first(d, yy):
        where = vg.at[0, block(yy, z)]
        return send(where, where, ys0.at[d - 1], yr0.at[d - 1], (((y + d) % ny) * nz + z, r))

    def ring0(way, k, d, incoming):
        yy = (y + ny - d) % ny
        if way == 0:
            zz = (z + 2 * nz - k - (1 if incoming else 0)) % nz
            to = right
        else:
            zz = (z + k + (1 if incoming else 0)) % nz
            to = left
        where = vg.at[0, block(yy, zz)]
        return send(where, where, zs0.at[way, k, d], zr0.at[way, k, d], (y * nz + to, r))

    def ring1(way, k, incoming):
        if way == 0:
            zz = (z + 2 * nz - k - (1 if incoming else 0)) % nz
            to = right
        else:
            zz = (z + k + (1 if incoming else 0)) % nz
            to = left
        where = vg.at[1, block(y, zz)]
        return send(where, where, zs1.at[way, k], zr1.at[way, k], (y * nz + to, r))

    def y_last(d, slot, zz, incoming):
        yy = (y + ny - d) % ny if incoming else y
        where = vg.at[1, block(yy, zz)]
        return send(
            where, where, ys1.at[d - 1, slot], yr1.at[d - 1, slot], (((y + d) % ny) * nz + z, r)
        )

    def slot_z(slot):
        return jnp.where(slot <= kr, z + nz - slot, z + slot - kr) % nz

    ways = ((0, kr), (1, kl))
    for d in range(1, ny):
        y_first(d, y).start()
    for way, steps in ways:
        if steps:
            ring0(way, 0, 0, False).start()
    for way, steps in ways:
        if steps:
            ring1(way, 0, False).start()
    for d in range(1, ny):
        y_last(d, 0, z, False).start()
    for d in range(1, ny):
        y_first(d, (y + ny - d) % ny).wait_recv()
        for way, steps in ways:
            if steps:
                ring0(way, 0, d, False).start()

    def ring_step(k, carry):
        for way, steps in ways:

            @pl.when(k < steps)
            def _(way=way, steps=steps):
                for d in range(ny):
                    ring0(way, k, d, True).wait_recv()

                    @pl.when(k + 1 < steps)
                    def _():
                        ring0(way, k + 1, d, False).start()

                ring1(way, k, True).wait_recv()

                @pl.when(k + 1 < steps)
                def _():
                    ring1(way, k + 1, False).start()

                slot = k + 1 + (kr if way else 0)
                zz = (z + 2 * nz - k - 1) % nz if way == 0 else (z + k + 1) % nz
                for d in range(1, ny):
                    y_last(d, slot, zz, False).start()

        return carry

    lax.fori_loop(0, kr, ring_step, 0)

    forward = one_hot((rank, rank), lambda i: (i % vw) * ow + i // vw)
    backward = one_hot((rank, rank), lambda i: (i % ow) * vw + i // ow)

    def exchange(c, d):
        to = (r + d) % nr
        return send(
            s_buf.at[c, to], x_buf.at[c, r], as_sem.at[c, d - 1], ar_sem.at[c, d - 1], (mode, to)
        )

    def exchange_from(c, d):
        source = (r + nr - d) % nr
        return send(
            s_buf.at[c, source], x_buf.at[c, source], as_sem.at[c, d - 1], ar_sem.at[c, d - 1],
            (mode, source),
        )

    def product(c):
        mt, nt = min(256, rows), min(256, ql * vw)

        def tile(n, carry):
            a = pl.ds(pl.multiple_of((n % (rows // mt)) * mt, mt), mt)
            b = pl.ds(pl.multiple_of((n // (rows // mt)) * nt, nt), nt)
            acc[a, b] = mm(o_buf[c, a, :], vg[c, :, b])
            return carry

        lax.fori_loop(0, (rows // mt) * (ql * vw // nt), tile, 0)

        def arrange(d, carry):
            to = (r + d) % nr
            base = to * (ow * chunk)
            for t in range(ow):
                strip = acc[pl.ds(pl.multiple_of(base + t * chunk, chunk), chunk), :].astype(BF16)
                for q in range(ql):
                    s_buf[c, to, q * chunk : (q + 1) * chunk, t * vw : (t + 1) * vw] = strip[
                        :, q * vw : (q + 1) * vw
                    ]

            @pl.when(d < nr)
            def _():
                exchange(c, d).start()

            return carry

        lax.fori_loop(1, nr + 1, arrange, 0)
        x_buf[c, r] = s_buf[c, r]

    def collect(c):
        def arrived(d, carry):
            exchange_from(c, d).wait_recv()
            return carry

        lax.fori_loop(1, nr, arrived, 0)
        per = ql * chunk
        lanes = min(128, rank)
        for source in range(nr):
            for h in range(rank // lanes):
                y_buf[h, source * per : (source + 1) * per, :] = x_buf[
                    c, source, :, h * lanes : (h + 1) * lanes
                ].astype(F32)
        bh, bl = split(b_ref[c + 1])
        for i in range(ni):
            raw = jnp.concatenate(
                [y_buf[h, pl.ds(i, rank, stride=ni), :] for h in range(rank // lanes)], axis=1
            ).astype(BF16)
            now = mm(raw, forward).astype(BF16)
            p_buf[i] = now
            pt_buf[i] = mm_nt(backward, raw).astype(BF16)
            q_out[c, i] = mm(now, bh) + mm(now, bl)

    def partial_gram(g):
        gh, gl = split(g)
        total = None
        for i in range(ni):
            now = p_buf[i]
            wh, wl = split(mm(gh, now) + mm(gl, now))
            flipped = pt_buf[i]
            term = mm(flipped, wh) + mm(flipped, wl)
            total = term if total is None else total + term
        part[...] = total * (1.0 / (modes * rank))

    def own_rows(index):
        return pl.ds(pl.multiple_of(index * rb_rows, rb_rows), rb_rows)

    def scatter(n, k):
        other, device = group(k)
        return send(part.at[own_rows(other)], ra.at[n, o], a_s.at[n, k - 1], a_r.at[n, k - 1], device)

    def along(n, k):
        return send(
            sb.at[n], rb.at[n, z], b_s.at[n, k - 1], b_r.at[n, k - 1],
            (y * nz + (z + k) % nz, r),
        )

    def spread(n, k):
        where = gram.at[n, own_rows(o)]
        return send(where, where, c_s.at[n, k - 1], c_r.at[n, k - 1], group(k)[1])

    def each(low, high, action):
        def body(k, carry):
            action(k)
            return carry

        lax.fori_loop(low, high, body, 0)

    def all_reduce(n):
        each(1, no, lambda k: scatter(n, k).start())
        ra[n, o] = part[own_rows(o), :]
        each(
            1, no,
            lambda k: send(
                ra.at[n, group_from(k)], ra.at[n, group_from(k)],
                a_s.at[n, k - 1], a_r.at[n, k - 1], group(k)[1],
            ).wait_recv(),
        )
        total = ra[n, 0]
        for k in range(1, no):
            total = total + ra[n, k]
        sb[n] = total
        rb[n, z] = total
        each(1, nz, lambda k: along(n, k).start())
        each(
            1, nz,
            lambda k: send(
                sb.at[n], rb.at[n, (z + nz - k) % nz], b_s.at[n, k - 1], b_r.at[n, k - 1],
                (y * nz + (z + k) % nz, r),
            ).wait_recv(),
        )
        total = rb[n, 0]
        for k in range(1, nz):
            total = total + rb[n, k]
        gram[n, own_rows(o), :] = total
        each(1, no, lambda k: spread(n, k).start())

        def landed(k):
            where = gram.at[n, own_rows(group_from(k))]
            send(where, where, c_s.at[n, k - 1], c_r.at[n, k - 1], group(k)[1]).wait_recv()

        each(1, no, landed)
        each(1, no, lambda k: scatter(n, k).wait_send())
        each(1, nz, lambda k: along(n, k).wait_send())
        each(1, no, lambda k: spread(n, k).wait_send())

    product(0)
    collect(0)
    partial_gram(g_ref[...])
    all_reduce(0)

    def y_arrived(slot):
        for d in range(1, ny):
            y_last(d, slot, slot_z(slot), True).wait_recv()

    each(0, nz, y_arrived)
    product(1)
    collect(1)
    partial_gram(gram[0])
    all_reduce(1)
    gram_out[...] = gram[...]

    for d in range(1, ny):
        y_first(d, y).wait_send()
    for way, steps in ways:
        if steps:

            def sent(k, way=way):
                for d in range(ny):
                    ring0(way, k, d, False).wait_send()
                ring1(way, k, False).wait_send()

            each(0, steps, sent)

    def y_sent(slot):
        for d in range(1, ny):
            y_last(d, slot, slot_z(slot), False).wait_send()

    each(0, nz, y_sent)
    for c in range(2):
        each(1, nr, lambda d, c=c: exchange(c, d).wait_send())


def shards(nr, nmode, operator_cores, vector_cores, left_gram, bases):
    cores, ow, _, lm, modes = operator_cores.shape
    ql, vw = vector_cores.shape[1:3]
    rank = left_gram.shape[0]
    ny = GRID_Y
    nz = nmode // ny
    ni = lm // nr
    rows = ow * ow * lm
    no = ny * nr
    rb_rows = rank // no
    kr = nz // 2
    dims = (ny, nz, nr, lm, ql, vw, ow, rank)
    dma = pltpu.SemaphoreType.DMA
    operator_rows = operator_cores.reshape(cores, rows, modes)
    vector_rows = vector_cores.reshape(cores, ql * vw, lm)
    vmem = pl.BlockSpec(memory_space=pltpu.VMEM)
    pieces, grams = pl.pallas_call(
        functools.partial(window_kernel, dims),
        out_shape=(
            jax.ShapeDtypeStruct((cores, ni, rank, bases.shape[2]), F32),
            jax.ShapeDtypeStruct((cores, rank, rank), F32),
        ),
        in_specs=[vmem, pl.BlockSpec(memory_space=pl.ANY), vmem, vmem],
        out_specs=(vmem, vmem),
        scratch_shapes=[
            pltpu.VMEM((cores, rows, modes), BF16),
            pltpu.VMEM((cores, modes, ql * vw), BF16),
            pltpu.VMEM((rows, ql * vw), F32),
            pltpu.VMEM((cores, nr, ql * ow * ni, rank), BF16),
            pltpu.VMEM((cores, nr, ql * ow * ni, rank), BF16),
            pltpu.VMEM((max(1, rank // 128), rank * ni, min(128, rank)), F32),
            pltpu.VMEM((ni, rank, rank), BF16),
            pltpu.VMEM((ni, rank, rank), BF16),
            pltpu.VMEM((rank, rank), F32),
            pltpu.VMEM((cores, no, rb_rows, rank), F32),
            pltpu.VMEM((cores, rb_rows, rank), F32),
            pltpu.VMEM((cores, nz, rb_rows, rank), F32),
            pltpu.VMEM((cores, rank, rank), F32),
            dma((2,)),
            dma((ny - 1,)), dma((ny - 1,)),
            dma((2, kr, ny)), dma((2, kr, ny)),
            dma((2, kr)), dma((2, kr)),
            dma((ny - 1, nz)), dma((ny - 1, nz)),
            dma((2, nr - 1)), dma((2, nr - 1)),
            dma((2, no - 1)), dma((2, no - 1)),
            dma((2, nz - 1)), dma((2, nz - 1)),
            dma((2, no - 1)), dma((2, no - 1)),
        ],
        compiler_params=pltpu.CompilerParams(collective_id=0, has_side_effects=True),
    )(vector_rows, operator_rows, left_gram, bases)
    results = []
    for core, gram_now in enumerate((left_gram, grams[0])):
        mixing = solve_mixing(gram_now, bases[core])
        results.append(
            jnp.einsum("ua,iav->uiv", mixing, pieces[core], precision=HIGHEST_PRECISION)
        )
    return (jnp.stack(results), grams[1])


def solution(mesh):
    placed = (P(None, None, None, "mode", None), P(None, "rank", None, "mode"), P(), P())
    return jax.shard_map(
        functools.partial(shards, mesh.shape["rank"], mesh.shape["mode"]),
        mesh=mesh,
        in_specs=placed,
        out_specs=(P(None, None, ("mode", "rank"), None), P()),
        check_vma=False,
    )
```

time: 1260 us -> 166 us (0.13)
  waiting for transfers between devices: 1160 us -> 0 us
  Pallas kernels: 0 us -> 129 us
  starting transfers between devices: 26.4 us -> 0 us
  local copies, waits for them, and re-layouts: 21.9 us -> 5.55 us
  matrix products: 19.1 us -> 5.8 us
  between operations: 14 us -> 0.81 us
    psum x2 -> x0, waiting for transfers between devices: 899 us -> none  [shards(): gram_now = lax.psum(partial_gram, ('mode', 'rank'))]
    all_gather x2 -> x0, waiting for transfers between devices: 251 us -> none  [shards(): gathered = lax.all_gather(vector_core, 'mode', axis=2, tiled=True)]
    pallas_call x0 -> x1, Pallas kernels: none -> 129 us  [shards(): pl.pallas_call(functools.partial(window_kernel, dims), out_shape=(jax.Sha...]
    all_to_all x2 -> x0, starting transfers between devices: 26.1 us -> none  [shards(): lax.all_to_all(row_major, 'rank', split_axis=1, concat_axis=0, tiled=True)]
  transfers between devices with their start and end apart: 6 -> 0, of which waited for: 5 -> 0; matrix products, arithmetic and copies ran while one was open for 4% -> 0% of each run, Pallas kernels for 0% -> 0%
where the time goes in v1:
time: 166 us
  Pallas kernels  129 us (78%)
  other arithmetic  24.2 us (15%)
  matrix products  5.8 us (3%)
  local copies, waits for them, and re-layouts  5.55 us (3%)
    pallas_call x1, Pallas kernels, shards(): pl.pallas_call(functools.partial(window_kernel, dims), out_shape=(jax.Sha...  129 us
    another operation x6, other arithmetic, solve_mixing(): lower_factor = jnp.linalg.cholesky(reduced)  13 us
    another operation x4, other arithmetic, solve_mixing(): return jax.scipy.linalg.cho_solve((lower_factor, True), projected)  11.1 us
    unnamed x9, local copies, waits for them, and re-layouts  4.53 us

profile of v1, /device:TPU:1, one launch (start us, length us, event | category | flops | bytes accessed | tf_op | source)
XLA Modules:
  0.0 165.9 jit_solution(2472942413043391982)
XLA Ops:
  0.6 0.0 copy-start.1
  0.6 0.0 copy-start
  0.7 1.8 %copy.8 = bf16[2,8,64,32]{3,2,1,0:T(8,128)(2,1)} copy(bf16[2,8,64,32]{2,3,1,0:T(8,128)(2,1)} %param.8) | data formatting | bytes 131072 | tf_op args[1]
  2.5 1.8 %copy.9.refs_3_ = f32[3,256,64]{2,1,0:T(8,128)} copy(f32[3,256,64]{1,2,0:T(8,128)} %param.10) | data formatting | bytes 393216 | tf_op args[3]
  4.3 129.5 %shard_map.59 = (f32[2,4,256,64]{3,2,1,0:T(8,128)}, f32[2,256,256]{2,1,0:T(8,128)}) custom-call(bf16[2,512,32]{2,1,0:T(8,128)(2,1)} %bitcast.73, bf16[2,512,2048]{2,1,0:T(8,128)(2,1)} %bitcast.72, f32[256,256]{1,0:T(8,128)} %refs_2_.1, f32[3,256,64]{2,1,0:T(8,128)} %copy.9.refs_3_), custom_call_target="tpu_custom_call" | custom-call | tf_op jit(solution)/shard_map/pallas_call | solution.py:404
  133.8 0.0 copy-start.2
  133.8 0.0 copy-done
  133.8 1.3 fusion.4
  135.1 0.2 fusion.9
  135.3 0.1 copy.11
  135.4 0.1 copy.12
  135.5 5.8 %cholesky.55 = f32[64,64]{1,0:T(8,128)S(1)} custom-call(f32[64,64]{1,0:T(8,128)S(1)} %fusion.24), custom_call_target="Cholesky" | custom-call | tf_op jit(solution)/shard_map/jit(cholesky)/cholesky | solution.py:25
  141.4 0.6 compare_reduce_fusion
  142.0 0.7 fusion.21
  142.7 4.9 %custom-call.9 = f32[1,64,64]{1,2,0:T(8,128)S(1)} custom-call(f32[1,64,64]{2,1,0:T(8,128)S(1)} %fusion.21), custom_call_target="InvertDiagBlocksLowerTriangular" | custom-call | tf_op jit(solution)/shard_map/jit(_cho_solve)/triangular_solve | solution.py:26
  147.6 0.3 fusion.7
  147.9 0.2 convolution_bitcast_fusion.2
  148.1 1.5 convolution_bitcast_fusion
  149.5 0.0 copy-done.1
  149.5 0.2 fusion.14
  149.8 0.2 fusion.12
  150.0 0.1 copy.6
  150.1 0.1 copy.7
  150.2 5.8 %cholesky.44 = f32[64,64]{1,0:T(8,128)S(1)} custom-call(f32[64,64]{1,0:T(8,128)S(1)} %fusion.29), custom_call_target="Cholesky" | custom-call | tf_op jit(solution)/shard_map/jit(cholesky)/cholesky | solution.py:25
  156.1 0.6 compare_reduce_fusion.1
  156.7 0.7 fusion.20
  157.4 4.9 %custom-call.8 = f32[1,64,64]{1,2,0:T(8,128)S(1)} custom-call(f32[1,64,64]{2,1,0:T(8,128)S(1)} %fusion.20), custom_call_target="InvertDiagBlocksLowerTriangular" | custom-call | tf_op jit(solution)/shard_map/jit(_cho_solve)/triangular_solve | solution.py:26
  162.3 0.3 fusion.27
  162.6 0.2 convolution_bitcast_fusion.3
  162.8 1.5 convolution_bitcast_fusion.1
  164.3 0.9 copy.14
  165.1 0.0 copy-done.2
  165.1 0.7 slice_bitcast_fusion
  (7 shorter events, 0.1 us)
Async XLA Ops:
  0.6 148.9 %copy-start.1 = (f32[256,256]{1,0:T(8,128)S(1)}, f32[256,256]{1,0:T(8,128)}, u32[]{:S(2)}) copy-start(f32[256,256]{1,0:T(8,128)} %refs_2_.1) | copy-start | bytes 786436
  0.6 133.2 %copy-start = (f32[3,256,64]{1,2,0:T(8,128)S(1)}, f32[3,256,64]{1,2,0:T(8,128)}, u32[]{:S(2)}) copy-start(f32[3,256,64]{1,2,0:T(8,128)} %param.10) | copy-start | bytes 589828
  133.8 31.3 %copy-start.2 = (f32[2,256,256]{2,1,0:T(8,128)S(1)}, f32[2,256,256]{2,1,0:T(8,128)}, u32[]{:S(2)}) copy-start(f32[2,256,256]{2,1,0:T(8,128)} %get-tuple-element.7) | copy-start | bytes 1572868

commit v2 on v1

--- a/solution.py
+++ b/solution.py
@@ -14,24 +14,14 @@
 BF16 = jnp.bfloat16
 
 
-def solve_mixing(gram_now, basis):
-    projected = jnp.dot(
-        basis.T, gram_now, precision=HIGHEST_PRECISION, preferred_element_type=jnp.float32
-    )
-    reduced = jnp.dot(
-        projected, basis, precision=HIGHEST_PRECISION, preferred_element_type=jnp.float32
-    )
-    reduced = 0.5 * (reduced + reduced.T)
-    lower_factor = jnp.linalg.cholesky(reduced)
-    return jax.scipy.linalg.cho_solve((lower_factor, True), projected)
-
-
 def mm(a, b):
     return jnp.dot(a, b, preferred_element_type=F32)
 
 
-def mm_nt(a, b):
-    return lax.dot_general(a, b, (((1,), (1,)), ((), ())), preferred_element_type=F32)
+def mm_nt(a, b, precision=None):
+    return lax.dot_general(
+        a, b, (((1,), (1,)), ((), ())), precision=precision, preferred_element_type=F32
+    )
 
 
 def split(a):
@@ -47,8 +37,8 @@
 
 def window_kernel(dims, *refs):
     (ny, nz, nr, lm, ql, vw, ow, rank) = dims
-    (v_ref, o_hbm, g_ref, b_ref, q_out, gram_out,
-     o_buf, vg, acc, s_buf, x_buf, y_buf, p_buf, pt_buf, part, ra, sb, rb, gram,
+    (v_ref, o_hbm, g_ref, b_ref, r_out, gram_out,
+     o_buf, vg, acc, s_buf, x_buf, y_buf, p_buf, pt_buf, q_buf, aug, part, ra, sb, rb, gram,
      o_sem, ys0, yr0, zs0, zr0, zs1, zr1, ys1, yr1, as_sem, ar_sem,
      a_s, a_r, b_s, b_r, c_s, c_r) = refs
     modes = ny * nz * lm
@@ -57,6 +47,8 @@
     chunk = ow * ni
     no = ny * nr
     rb_rows = rank // no
+    u_rank = b_ref.shape[1]
+    head = aug.shape[1] - rank
     kr = nz // 2
     kl = nz - 1 - kr
     mode = lax.axis_index("mode")
@@ -97,9 +89,9 @@
     def block(yy, zz):
         return pl.ds(pl.multiple_of((yy * nz + zz) * lm, lm), lm)
 
-    eye = one_hot((lm, lm), lambda i: i)
     for c in range(2):
-        vg[c, block(y, z), :] = mm_nt(eye, v_ref[c]).astype(BF16)
+        for q in range(ql):
+            vg[c, block(y, z), q * vw : (q + 1) * vw] = v_ref[c, q]
 
     def operator_row(i):
         rr, rest = i // (ow * chunk), i % (ow * chunk)
@@ -273,7 +265,7 @@
             now = mm(raw, forward).astype(BF16)
             p_buf[i] = now
             pt_buf[i] = mm_nt(backward, raw).astype(BF16)
-            q_out[c, i] = mm(now, bh) + mm(now, bl)
+            q_buf[c, :, i * u_rank : (i + 1) * u_rank] = mm_nt(now, bh) + mm_nt(now, bl)
 
     def partial_gram(g):
         gh, gl = split(g)
@@ -310,8 +302,45 @@
 
         lax.fori_loop(low, high, body, 0)
 
-    def all_reduce(n):
+    def solve_start(c, g):
+        basis = b_ref[c]
+        projected = jnp.dot(
+            basis, g, precision=HIGHEST_PRECISION, preferred_element_type=F32
+        )
+        reduced = mm_nt(projected, basis, HIGHEST_PRECISION)
+        aug[:, :head] = jnp.zeros((u_rank, head), F32)
+        aug[:, :u_rank] = 0.5 * (reduced + reduced.T)
+        aug[:, head:] = projected
+
+    def solve_steps(low, high):
+        row_index = lax.broadcasted_iota(jnp.int32, (u_rank, 1), 0)
+        lane_index = lax.broadcasted_iota(jnp.int32, (u_rank, head), 1)
+
+        def step(k):
+            row = aug[pl.ds(k, 1), :]
+            chosen = lane_index == k
+            column = jnp.sum(
+                jnp.where(chosen, aug[:, :head], 0.0), axis=1, keepdims=True
+            )
+            pivot = jnp.sum(
+                jnp.where(chosen[:1], row[:, :head], 0.0), axis=1, keepdims=True
+            )
+            scaled = row / pivot
+            aug[...] = aug[...] - jnp.where(row_index == k, 0.0, column) * scaled
+            aug[pl.ds(k, 1), :] = scaled
+
+        each(low, high, step)
+
+    def solve_end(c):
+        mh, ml = split(aug[:, head:])
+        for i in range(ni):
+            qh, ql_ = split(q_buf[c, :, i * u_rank : (i + 1) * u_rank])
+            r_out[c, i] = mm(mh, qh) + (mm(mh, ql_) + mm(ml, qh))
+
+    def all_reduce(n, g):
         each(1, no, lambda k: scatter(n, k).start())
+        solve_start(n, g)
+        solve_steps(0, u_rank // 4)
         ra[n, o] = part[own_rows(o), :]
         each(
             1, no,
@@ -326,6 +355,7 @@
         sb[n] = total
         rb[n, z] = total
         each(1, nz, lambda k: along(n, k).start())
+        solve_steps(u_rank // 4, u_rank)
         each(
             1, nz,
             lambda k: send(
@@ -338,6 +368,7 @@
             total = total + rb[n, k]
         gram[n, own_rows(o), :] = total
         each(1, no, lambda k: spread(n, k).start())
+        solve_end(n)
 
         def landed(k):
             where = gram.at[n, own_rows(group_from(k))]
@@ -351,7 +382,7 @@
     product(0)
     collect(0)
     partial_gram(g_ref[...])
-    all_reduce(0)
+    all_reduce(0, g_ref[...])
 
     def y_arrived(slot):
         for d in range(1, ny):
@@ -361,8 +392,8 @@
     product(1)
     collect(1)
     partial_gram(gram[0])
-    all_reduce(1)
-    gram_out[...] = gram[...]
+    all_reduce(1, gram[0])
+    gram_out[...] = gram[1]
 
     for d in range(1, ny):
         y_first(d, y).wait_send()
@@ -399,13 +430,15 @@
     dims = (ny, nz, nr, lm, ql, vw, ow, rank)
     dma = pltpu.SemaphoreType.DMA
     operator_rows = operator_cores.reshape(cores, rows, modes)
-    vector_rows = vector_cores.reshape(cores, ql * vw, lm)
+    vector_rows = vector_cores.transpose(0, 1, 3, 2)
+    bases_rows = bases.transpose(0, 2, 1)
+    out_rank = bases.shape[2]
     vmem = pl.BlockSpec(memory_space=pltpu.VMEM)
-    pieces, grams = pl.pallas_call(
+    pieces, gram = pl.pallas_call(
         functools.partial(window_kernel, dims),
         out_shape=(
-            jax.ShapeDtypeStruct((cores, ni, rank, bases.shape[2]), F32),
-            jax.ShapeDtypeStruct((cores, rank, rank), F32),
+            jax.ShapeDtypeStruct((cores, ni, out_rank, out_rank), F32),
+            jax.ShapeDtypeStruct((rank, rank), F32),
         ),
         in_specs=[vmem, pl.BlockSpec(memory_space=pl.ANY), vmem, vmem],
         out_specs=(vmem, vmem),
@@ -418,6 +451,8 @@
             pltpu.VMEM((max(1, rank // 128), rank * ni, min(128, rank)), F32),
             pltpu.VMEM((ni, rank, rank), BF16),
             pltpu.VMEM((ni, rank, rank), BF16),
+            pltpu.VMEM((cores, rank, ni * out_rank), F32),
+            pltpu.VMEM((out_rank, 128 + rank), F32),
             pltpu.VMEM((rank, rank), F32),
             pltpu.VMEM((cores, no, rb_rows, rank), F32),
             pltpu.VMEM((cores, rb_rows, rank), F32),
@@ -434,14 +469,8 @@
             dma((2, no - 1)), dma((2, no - 1)),
         ],
         compiler_params=pltpu.CompilerParams(collective_id=0, has_side_effects=True),
-    )(vector_rows, operator_rows, left_gram, bases)
-    results = []
-    for core, gram_now in enumerate((left_gram, grams[0])):
-        mixing = solve_mixing(gram_now, bases[core])
-        results.append(
-            jnp.einsum("ua,iav->uiv", mixing, pieces[core], precision=HIGHEST_PRECISION)
-        )
-    return (jnp.stack(results), grams[1])
+    )(vector_rows, operator_rows, left_gram, bases_rows)
+    return (pieces.transpose(0, 2, 1, 3), gram)
 
 
 def solution(mesh):

time: 166 us -> 133 us (0.80)
  other arithmetic: 24.2 us -> 0 us
  matrix products: 5.8 us -> 0 us
  local copies, waits for them, and re-layouts: 5.55 us -> 3.49 us
    another operation x11 -> x0, other arithmetic: 24.2 us -> none  [the longest x6 13 us: solve_mixing(): lower_factor = jnp.linalg.cholesky(reduced)]
    dot_general x6 -> x0, matrix products: 4.88 us -> none  [the longest x2 2.95 us: shards(): jnp.einsum('ua,iav->uiv', mixing, pieces[core], precision=HIGHEST_PRECISION)]
    unnamed x9 -> x2, local copies, waits for them, and re-layouts: 4.53 us -> 3.49 us
where the time goes in v2:
time: 133 us
  Pallas kernels  128 us (96%)
  local copies, waits for them, and re-layouts  3.49 us (3%)
    pallas_call x1, Pallas kernels, shards(): pl.pallas_call(functools.partial(window_kernel, dims), out_shape=(jax.Sha...  128 us
    unnamed x2, local copies, waits for them, and re-layouts  3.49 us

profile of v2, /device:TPU:1, one launch (start us, length us, event | category | flops | bytes accessed | tf_op | source)
XLA Modules:
  0.0 132.5 jit_solution(6869615790676882996)
XLA Ops:
  0.6 128.4 %shard_map.59 = (f32[2,4,64,64]{3,2,1,0:T(8,128)}, f32[256,256]{1,0:T(8,128)}) custom-call(bf16[2,8,32,64]{3,2,1,0:T(8,128)(2,1)} %bitcast.7, bf16[2,512,2048]{2,1,0:T(8,128)(2,1)} %bitcast.4, f32[256,256]{1,0:T(8,128)} %refs_2_.1, f32[3,64,256]{2,1,0:T(8,128)} %bitcast.6), custom_call_target="tpu_custom_call" | custom-call | tf_op jit(solution)/shard_map/pallas_call | solution.py:437
  129.0 1.8 %copy.6 = f32[2,64,4,64]{3,2,1,0:T(4,128)} copy(f32[2,64,4,64]{3,1,2,0:T(8,128)} %bitcast.5) | data formatting | bytes 262144
  130.9 1.7 %copy.8 = f32[256,256]{1,0:T(8,128)} copy(f32[256,256]{1,0:T(8,128)} %get-tuple-element.11) | data formatting | bytes 524288

commit v3 on v2

--- a/solution.py
+++ b/solution.py
@@ -49,6 +49,7 @@
     rb_rows = rank // no
     u_rank = b_ref.shape[1]
     head = aug.shape[1] - rank
+    cut = ql * vw // 4
     kr = nz // 2
     kl = nz - 1 - kr
     mode = lax.axis_index("mode")
@@ -120,58 +121,70 @@
         )
 
     def y_first(d, yy):
-        where = vg.at[0, block(yy, z)]
+        where = vg.at[0, block(yy, z), :cut]
         return send(where, where, ys0.at[d - 1], yr0.at[d - 1], (((y + d) % ny) * nz + z, r))
 
+    def towards(way, k, incoming):
+        ahead = 1 if incoming else 0
+        if way == 0:
+            return (z + 2 * nz - k - ahead) % nz, right
+        return (z + k + ahead) % nz, left
+
     def ring0(way, k, d, incoming):
-        yy = (y + ny - d) % ny
-        if way == 0:
-            zz = (z + 2 * nz - k - (1 if incoming else 0)) % nz
-            to = right
-        else:
-            zz = (z + k + (1 if incoming else 0)) % nz
-            to = left
-        where = vg.at[0, block(yy, zz)]
+        zz, to = towards(way, k, incoming)
+        where = vg.at[0, block((y + ny - d) % ny, zz), :cut]
         return send(where, where, zs0.at[way, k, d], zr0.at[way, k, d], (y * nz + to, r))
 
-    def ring1(way, k, incoming):
-        if way == 0:
-            zz = (z + 2 * nz - k - (1 if incoming else 0)) % nz
-            to = right
-        else:
-            zz = (z + k + (1 if incoming else 0)) % nz
-            to = left
-        where = vg.at[1, block(y, zz)]
-        return send(where, where, zs1.at[way, k], zr1.at[way, k], (y * nz + to, r))
-
-    def y_last(d, slot, zz, incoming):
-        yy = (y + ny - d) % ny if incoming else y
-        where = vg.at[1, block(yy, zz)]
+    def part_of(c, yy, zz):
+        if c == 0:
+            return vg.at[0, block(yy, zz), cut:]
+        return vg.at[1, block(yy, zz)]
+
+    def ring1(c, way, k, incoming):
+        zz, to = towards(way, k, incoming)
+        where = part_of(c, y, zz)
+        return send(where, where, zs1.at[c, way, k], zr1.at[c, way, k], (y * nz + to, r))
+
+    def y_last(c, d, slot, zz, incoming):
+        where = part_of(c, (y + ny - d) % ny if incoming else y, zz)
         return send(
-            where, where, ys1.at[d - 1, slot], yr1.at[d - 1, slot], (((y + d) % ny) * nz + z, r)
+            where, where, ys1.at[c, d - 1, slot], yr1.at[c, d - 1, slot],
+            (((y + d) % ny) * nz + z, r),
         )
 
     def slot_z(slot):
         return jnp.where(slot <= kr, z + nz - slot, z + slot - kr) % nz
 
-    ways = ((0, kr), (1, kl))
+    ways = tuple((way, steps) for way, steps in ((0, kr), (1, kl)) if steps)
+    for way, steps in ways:
+        ring1(0, way, 0, False).start()
     for d in range(1, ny):
         y_first(d, y).start()
     for way, steps in ways:
-        if steps:
-            ring0(way, 0, 0, False).start()
+        ring0(way, 0, 0, False).start()
+    for d in range(1, ny):
+        y_last(0, d, 0, z, False).start()
     for way, steps in ways:
-        if steps:
-            ring1(way, 0, False).start()
-    for d in range(1, ny):
-        y_last(d, 0, z, False).start()
+        ring1(1, way, 0, False).start()
     for d in range(1, ny):
         y_first(d, (y + ny - d) % ny).wait_recv()
         for way, steps in ways:
-            if steps:
-                ring0(way, 0, d, False).start()
+            ring0(way, 0, d, False).start()
 
     def ring_step(k, carry):
+        for way, steps in ways:
+
+            @pl.when(k < steps)
+            def _(way=way, steps=steps):
+                ring1(0, way, k, True).wait_recv()
+
+                @pl.when(k + 1 < steps)
+                def _():
+                    ring1(0, way, k + 1, False).start()
+
+                for d in range(1, ny):
+                    y_last(0, d, k + 1 + (kr if way else 0), towards(way, k, True)[0], False).start()
+
         for way, steps in ways:
 
             @pl.when(k < steps)
@@ -183,20 +196,33 @@
                     def _():
                         ring0(way, k + 1, d, False).start()
 
-                ring1(way, k, True).wait_recv()
+                ring1(1, way, k, True).wait_recv()
 
                 @pl.when(k + 1 < steps)
                 def _():
-                    ring1(way, k + 1, False).start()
-
-                slot = k + 1 + (kr if way else 0)
-                zz = (z + 2 * nz - k - 1) % nz if way == 0 else (z + k + 1) % nz
-                for d in range(1, ny):
-                    y_last(d, slot, zz, False).start()
+                    ring1(1, way, k + 1, False).start()
 
         return carry
 
     lax.fori_loop(0, kr, ring_step, 0)
+
+    def y_arrived(c, slot):
+        for d in range(1, ny):
+            y_last(c, d, slot, slot_z(slot), True).wait_recv()
+
+    def y_pass(slot):
+        for d in range(1, ny):
+            y_last(1, d, slot, slot_z(slot), False).start()
+
+    def each(low, high, action):
+        def body(k, carry):
+            action(k)
+            return carry
+
+        lax.fori_loop(low, high, body, 0)
+
+    each(0, nz, functools.partial(y_arrived, 0))
+    each(0, nz, y_pass)
 
     forward = one_hot((rank, rank), lambda i: (i % vw) * ow + i // vw)
     backward = one_hot((rank, rank), lambda i: (i % ow) * vw + i // ow)
@@ -295,13 +321,6 @@
         where = gram.at[n, own_rows(o)]
         return send(where, where, c_s.at[n, k - 1], c_r.at[n, k - 1], group(k)[1])
 
-    def each(low, high, action):
-        def body(k, carry):
-            action(k)
-            return carry
-
-        lax.fori_loop(low, high, body, 0)
-
     def solve_start(c, g):
         basis = b_ref[c]
         projected = jnp.dot(
@@ -335,12 +354,11 @@
         mh, ml = split(aug[:, head:])
         for i in range(ni):
             qh, ql_ = split(q_buf[c, :, i * u_rank : (i + 1) * u_rank])
-            r_out[c, i] = mm(mh, qh) + (mm(mh, ql_) + mm(ml, qh))
-
-    def all_reduce(n, g):
+            r_out[c, :, i, :] = mm(mh, qh) + (mm(mh, ql_) + mm(ml, qh))
+
+    def all_reduce(n, fill_a, fill_b, fill_c):
         each(1, no, lambda k: scatter(n, k).start())
-        solve_start(n, g)
-        solve_steps(0, u_rank // 4)
+        fill_a()
         ra[n, o] = part[own_rows(o), :]
         each(
             1, no,
@@ -355,7 +373,7 @@
         sb[n] = total
         rb[n, z] = total
         each(1, nz, lambda k: along(n, k).start())
-        solve_steps(u_rank // 4, u_rank)
+        fill_b()
         each(
             1, nz,
             lambda k: send(
@@ -368,7 +386,7 @@
             total = total + rb[n, k]
         gram[n, own_rows(o), :] = total
         each(1, no, lambda k: spread(n, k).start())
-        solve_end(n)
+        fill_c()
 
         def landed(k):
             where = gram.at[n, own_rows(group_from(k))]
@@ -379,37 +397,45 @@
         each(1, nz, lambda k: along(n, k).wait_send())
         each(1, no, lambda k: spread(n, k).wait_send())
 
+    def solve_first():
+        solve_start(0, g_ref[...])
+        solve_steps(0, u_rank)
+        solve_end(0)
+
+    def product_second():
+        each(0, nz, functools.partial(y_arrived, 1))
+        product(1)
+
+    def solve_second():
+        solve_start(1, gram[0])
+        solve_steps(0, u_rank // 4)
+
     product(0)
     collect(0)
     partial_gram(g_ref[...])
-    all_reduce(0, g_ref[...])
-
-    def y_arrived(slot):
-        for d in range(1, ny):
-            y_last(d, slot, slot_z(slot), True).wait_recv()
-
-    each(0, nz, y_arrived)
-    product(1)
-    collect(1)
+    all_reduce(0, solve_first, product_second, lambda: collect(1))
     partial_gram(gram[0])
-    all_reduce(1, gram[0])
+    all_reduce(
+        1, solve_second, lambda: solve_steps(u_rank // 4, u_rank), lambda: solve_end(1)
+    )
     gram_out[...] = gram[1]
 
     for d in range(1, ny):
         y_first(d, y).wait_send()
     for way, steps in ways:
-        if steps:
-
-            def sent(k, way=way):
-                for d in range(ny):
-                    ring0(way, k, d, False).wait_send()
-                ring1(way, k, False).wait_send()
-
-            each(0, steps, sent)
+
+        def sent(k, way=way):
+            for d in range(ny):
+                ring0(way, k, d, False).wait_send()
+            for c in range(2):
+                ring1(c, way, k, False).wait_send()
+
+        each(0, steps, sent)
 
     def y_sent(slot):
-        for d in range(1, ny):
-            y_last(d, slot, slot_z(slot), False).wait_send()
+        for c in range(2):
+            for d in range(1, ny):
+                y_last(c, d, slot, slot_z(slot), False).wait_send()
 
     each(0, nz, y_sent)
     for c in range(2):
@@ -437,7 +463,7 @@
     pieces, gram = pl.pallas_call(
         functools.partial(window_kernel, dims),
         out_shape=(
-            jax.ShapeDtypeStruct((cores, ni, out_rank, out_rank), F32),
+            jax.ShapeDtypeStruct((cores, out_rank, ni, out_rank), F32),
             jax.ShapeDtypeStruct((rank, rank), F32),
         ),
         in_specs=[vmem, pl.BlockSpec(memory_space=pl.ANY), vmem, vmem],
@@ -461,8 +487,8 @@
             dma((2,)),
             dma((ny - 1,)), dma((ny - 1,)),
             dma((2, kr, ny)), dma((2, kr, ny)),
-            dma((2, kr)), dma((2, kr)),
-            dma((ny - 1, nz)), dma((ny - 1, nz)),
+            dma((2, 2, kr)), dma((2, 2, kr)),
+            dma((2, ny - 1, nz)), dma((2, ny - 1, nz)),
             dma((2, nr - 1)), dma((2, nr - 1)),
             dma((2, no - 1)), dma((2, no - 1)),
             dma((2, nz - 1)), dma((2, nz - 1)),
@@ -470,7 +496,7 @@
         ],
         compiler_params=pltpu.CompilerParams(collective_id=0, has_side_effects=True),
     )(vector_rows, operator_rows, left_gram, bases_rows)
-    return (pieces.transpose(0, 2, 1, 3), gram)
+    return pieces, gram
 
 
 def solution(mesh):

time: 133 us -> 127 us (0.955)
  Pallas kernels: 128 us -> 123 us
    pallas_call x1, Pallas kernels: 128 us -> 123 us  [shards(): pl.pallas_call(functools.partial(window_kernel, dims), out_shape=(jax.Sha...]
where the time goes in v3:
time: 127 us
  Pallas kernels  123 us (97%)
  local copies, waits for them, and re-layouts  3.34 us (3%)
    pallas_call x1, Pallas kernels, shards(): pl.pallas_call(functools.partial(window_kernel, dims), out_shape=(jax.Sha...  123 us
    unnamed x2, local copies, waits for them, and re-layouts  3.34 us

profile of v3, /device:TPU:1, one launch (start us, length us, event | category | flops | bytes accessed | tf_op | source)
XLA Modules:
  0.0 127.2 jit_solution(17247354658428096635)
XLA Ops:
  0.6 123.3 %shard_map.59 = (f32[2,64,4,64]{3,2,1,0:T(4,128)}, f32[256,256]{1,0:T(8,128)}) custom-call(bf16[2,8,32,64]{3,2,1,0:T(8,128)(2,1)} %bitcast.5, bf16[2,512,2048]{2,1,0:T(8,128)(2,1)} %bitcast.3, f32[256,256]{1,0:T(8,128)} %refs_2_.1, f32[3,64,256]{2,1,0:T(8,128)} %bitcast.4), custom_call_target="tpu_custom_call" | custom-call | tf_op jit(solution)/shard_map/pallas_call | solution.py:463
  123.9 1.7 %copy.8 = f32[2,64,4,64]{3,2,1,0:T(4,128)} copy(f32[2,64,4,64]{3,2,1,0:T(4,128)} %get-tuple-element.4) | data formatting | bytes 262144
  125.6 1.7 %copy.9 = f32[256,256]{1,0:T(8,128)} copy(f32[256,256]{1,0:T(8,128)} %get-tuple-element.5) | data formatting | bytes 524288

commit v4 on v3

--- a/solution.py
+++ b/solution.py
@@ -52,6 +52,7 @@
     cut = ql * vw // 4
     kr = nz // 2
     kl = nz - 1 - kr
+    direct = (1, ny - 1)
     mode = lax.axis_index("mode")
     r = lax.axis_index("rank")
     y = mode // nz
@@ -151,6 +152,19 @@
             where, where, ys1.at[c, d - 1, slot], yr1.at[c, d - 1, slot],
             (((y + d) % ny) * nz + z, r),
         )
+
+    def relay(c, slot):
+        step = jnp.where(slot % 2 == 0, 1, ny - 1)
+        where = part_of(c, (y + ny - step) % ny, slot_z(slot))
+        return send(
+            where, where, ys1.at[c, 1, slot], yr1.at[c, 1, slot],
+            (((y + step) % ny) * nz + z, r),
+        )
+
+    def relay_on(c, slot):
+        for d in direct:
+            y_last(c, d, slot, slot_z(slot), True).wait_recv()
+        relay(c, slot).start()
 
     def slot_z(slot):
         return jnp.where(slot <= kr, z + nz - slot, z + slot - kr) % nz
@@ -162,7 +176,7 @@
         y_first(d, y).start()
     for way, steps in ways:
         ring0(way, 0, 0, False).start()
-    for d in range(1, ny):
+    for d in direct:
         y_last(0, d, 0, z, False).start()
     for way, steps in ways:
         ring1(1, way, 0, False).start()
@@ -182,7 +196,7 @@
                 def _():
                     ring1(0, way, k + 1, False).start()
 
-                for d in range(1, ny):
+                for d in direct:
                     y_last(0, d, k + 1 + (kr if way else 0), towards(way, k, True)[0], False).start()
 
         for way, steps in ways:
@@ -202,16 +216,22 @@
                 def _():
                     ring1(1, way, k + 1, False).start()
 
+        relay_on(0, k)
+
+        @pl.when((k >= 1) & (k <= kl))
+        def _():
+            relay_on(0, k + kr)
+
         return carry
 
     lax.fori_loop(0, kr, ring_step, 0)
+    relay_on(0, kr)
 
     def y_arrived(c, slot):
-        for d in range(1, ny):
-            y_last(c, d, slot, slot_z(slot), True).wait_recv()
+        y_last(c, 2, slot, slot_z(slot), True).wait_recv()
 
     def y_pass(slot):
-        for d in range(1, ny):
+        for d in direct:
             y_last(1, d, slot, slot_z(slot), False).start()
 
     def each(low, high, action):
@@ -398,6 +418,7 @@
         each(1, no, lambda k: spread(n, k).wait_send())
 
     def solve_first():
+        each(0, nz, functools.partial(relay_on, 1))
         solve_start(0, g_ref[...])
         solve_steps(0, u_rank)
         solve_end(0)
@@ -434,8 +455,9 @@
 
     def y_sent(slot):
         for c in range(2):
-            for d in range(1, ny):
+            for d in direct:
                 y_last(c, d, slot, slot_z(slot), False).wait_send()
+            relay(c, slot).wait_send()
 
     each(0, nz, y_sent)
     for c in range(2):

time: 127 us -> 126 us (level)
  Pallas kernels: 123 us -> 121 us
    pallas_call x1, Pallas kernels: 123 us -> 121 us  [shards(): pl.pallas_call(functools.partial(window_kernel, dims), out_shape=(jax.Sha...]
where the time goes in v4:
time: 126 us; the launch traced here: 125 us
  Pallas kernels  121 us (96%)
  local copies, waits for them, and re-layouts  3.34 us (3%)
    pallas_call x1, Pallas kernels, shards(): pl.pallas_call(functools.partial(window_kernel, dims), out_shape=(jax.Sha...  121 us
    unnamed x2, local copies, waits for them, and re-layouts  3.34 us

profile of v4, /device:TPU:1, one launch (start us, length us, event | category | flops | bytes accessed | tf_op | source)
XLA Modules:
  0.0 125.4 jit_solution(13895212301357266801)
XLA Ops:
  0.6 121.5 %shard_map.59 = (f32[2,64,4,64]{3,2,1,0:T(4,128)}, f32[256,256]{1,0:T(8,128)}) custom-call(bf16[2,8,32,64]{3,2,1,0:T(8,128)(2,1)} %bitcast.5, bf16[2,512,2048]{2,1,0:T(8,128)(2,1)} %bitcast.3, f32[256,256]{1,0:T(8,128)} %refs_2_.1, f32[3,64,256]{2,1,0:T(8,128)} %bitcast.4), custom_call_target="tpu_custom_call" | custom-call | tf_op jit(solution)/shard_map/pallas_call | solution.py:485
  122.1 1.7 %copy.8 = f32[2,64,4,64]{3,2,1,0:T(4,128)} copy(f32[2,64,4,64]{3,2,1,0:T(4,128)} %get-tuple-element.4) | data formatting | bytes 262144
  123.8 1.7 %copy.9 = f32[256,256]{1,0:T(8,128)} copy(f32[256,256]{1,0:T(8,128)} %get-tuple-element.5) | data formatting | bytes 524288

commit v5 on v4

--- a/solution.py
+++ b/solution.py
@@ -103,10 +103,11 @@
 
     width = min(256, modes)
     order = one_hot((rows, rows), operator_row)
-    for c in range(2):
+
+    def reorder_operator(c):
         o_copies[c].wait()
 
-        def reorder(n, carry, c=c):
+        def reorder(n, carry):
             columns = pl.ds(pl.multiple_of(n * width, width), width)
             o_buf[c, :, columns] = mm(order, o_buf[c, :, columns]).astype(BF16)
             return carry
@@ -424,6 +425,7 @@
         solve_end(0)
 
     def product_second():
+        reorder_operator(1)
         each(0, nz, functools.partial(y_arrived, 1))
         product(1)
 
@@ -431,6 +433,7 @@
         solve_start(1, gram[0])
         solve_steps(0, u_rank // 4)
 
+    reorder_operator(0)
     product(0)
     collect(0)
     partial_gram(g_ref[...])

time: 126 us -> 127 us (level)
  Pallas kernels: 121 us -> 123 us
    pallas_call x1, Pallas kernels: 121 us -> 123 us  [shards(): pl.pallas_call(functools.partial(window_kernel, dims), out_shape=(jax.Sha...]
where the time goes in v5:
time: 127 us
  Pallas kernels  123 us (97%)
  local copies, waits for them, and re-layouts  3.34 us (3%)
    pallas_call x1, Pallas kernels, shards(): pl.pallas_call(functools.partial(window_kernel, dims), out_shape=(jax.Sha...  123 us
    unnamed x2, local copies, waits for them, and re-layouts  3.34 us

profile of v5, /device:TPU:1, one launch (start us, length us, event | category | flops | bytes accessed | tf_op | source)
XLA Modules:
  0.0 127.2 jit_solution(17225688480500274864)
XLA Ops:
  0.6 123.3 %shard_map.59 = (f32[2,64,4,64]{3,2,1,0:T(4,128)}, f32[256,256]{1,0:T(8,128)}) custom-call(bf16[2,8,32,64]{3,2,1,0:T(8,128)(2,1)} %bitcast.5, bf16[2,512,2048]{2,1,0:T(8,128)(2,1)} %bitcast.3, f32[256,256]{1,0:T(8,128)} %refs_2_.1, f32[3,64,256]{2,1,0:T(8,128)} %bitcast.4), custom_call_target="tpu_custom_call" | custom-call | tf_op jit(solution)/shard_map/pallas_call | solution.py:488
  123.9 1.7 %copy.8 = f32[2,64,4,64]{3,2,1,0:T(4,128)} copy(f32[2,64,4,64]{3,2,1,0:T(4,128)} %get-tuple-element.4) | data formatting | bytes 262144
  125.6 1.7 %copy.9 = f32[256,256]{1,0:T(8,128)} copy(f32[256,256]{1,0:T(8,128)} %get-tuple-element.5) | data formatting | bytes 524288
